TPU v7x, 32 devices: a whole 2x2x4 slice. The times are simulated.
32 devices in a mesh: expert: 8 (over z, x), dp: 4 (over y, core).
Axes of the slice: x: 2, y: 2, z: 4, core: 2. Of those that a mesh axis runs over, the one named last changes fastest.
Arguments:
- tokens: bfloat16 [1024, 7168], P('expert'), may hold values from -6 to 6
- routes: int32 [1024, 2], P('expert'), may hold values from 0 to 7, all different within a row; in each aligned block of 128 rows (0 to 127, 128 to 255, ...) at most 96 rows name the same one
- route_gates: bfloat16 [1024, 2], P('expert'), may hold values from 0.049804688 to 1
- cotangent: bfloat16 [1024, 7168], P('expert'), may hold values from -6 to 6
- weight_gate: bfloat16 [8, 7168, 1024], P('expert', None, 'dp'), may hold values from -0.0625 to 0.0625
- weight_up: bfloat16 [8, 7168, 1024], P('expert', None, 'dp'), may hold values from -0.0625 to 0.0625
- weight_down: bfloat16 [8, 1024, 7168], P('expert', 'dp'), may hold values from -0.1875 to 0.1875
Outputs:
- grad_tokens: bfloat16 [1024, 7168], P('expert', 'dp')
- grad_gate: bfloat16 [8, 7168, 1024], P('expert', None, 'dp')
- grad_up: bfloat16 [8, 7168, 1024], P('expert', None, 'dp')
- grad_down: bfloat16 [8, 1024, 7168], P('expert', 'dp')
Inputs may be any that keep to these rules, and one draw needn't show every extreme that they name: `routes`: within each aligned block of 128 rows (the tokens of one index of the expert axis) every row names 2 different experts and no expert is named by more than 96 rows; in every draw some block names some expert exactly 96 times.
All inputs are finite; a program needn't handle non-finite values.
Results may differ from a plain program's by a relative error of at most 0.011.
Values may be sent and summed in bfloat16 or wider, within the bound.
A program may use at most 192 MiB of HBM per device.

v0:
```python
import jax
import jax.numpy as jnp
from jax import lax
from jax.sharding import PartitionSpec as P


def slot_layout(routes, experts, capacity):
    flat_routes = routes.reshape(-1)
    onehot = (flat_routes[:, None] == jnp.arange(experts, dtype=jnp.int32)[None, :]).astype(
        jnp.int32
    )
    before = jnp.cumsum(onehot, axis=0) - onehot
    position = jnp.sum(before * onehot, axis=1)
    slot_index = flat_routes * capacity + position
    total_slots = flat_routes.shape[0]
    owners = (
        jnp.full((experts * capacity,), total_slots, dtype=jnp.int32)
        .at[slot_index]
        .set(jnp.arange(total_slots, dtype=jnp.int32))
    )
    return (slot_index, owners)


def pad_rows(source_array, owners, top_count):
    extended = jnp.concatenate(
        [source_array, jnp.zeros((1,) + source_array.shape[1:], source_array.dtype)], 0
    )
    return extended[owners // top_count]


def per_device(tokens, routes, route_gates, cotangent, weight_gate, weight_up, weight_down):
    members = lax.axis_size("expert")
    groups = lax.axis_size("dp")
    local_experts = weight_gate.shape[0]
    experts = members * local_experts
    token_rows = routes.shape[0]
    top_count = routes.shape[1]
    width = tokens.shape[1]
    quarter = width // groups
    capacity = 3 * token_rows * top_count // experts
    slot_index, owners = slot_layout(routes, experts, capacity)
    gate_flat = jnp.concatenate([route_gates.reshape(-1), jnp.zeros((1,), route_gates.dtype)], 0)
    gate_send = gate_flat[owners].reshape(experts, capacity)
    token_send = pad_rows(tokens, owners, top_count).reshape(experts, capacity, width)
    back_send = pad_rows(cotangent, owners, top_count).reshape(experts, capacity, width)
    token_arrived, back_arrived, gate_arrived = (
        lax.all_to_all(token_send, "expert", split_axis=0, concat_axis=1, tiled=True),
        lax.all_to_all(back_send, "expert", split_axis=0, concat_axis=1, tiled=True),
        lax.all_to_all(gate_send, "expert", split_axis=0, concat_axis=1, tiled=True),
    )
    scale = gate_arrived.astype(jnp.float32)[:, :, None]
    pre_gate = jnp.einsum(
        "erd,edf->erf", token_arrived, weight_gate, preferred_element_type=jnp.float32
    )
    pre_up = jnp.einsum(
        "erd,edf->erf", token_arrived, weight_up, preferred_element_type=jnp.float32
    )
    sigma = jax.nn.sigmoid(pre_gate)
    activated = pre_gate * sigma
    scaled_hidden = (scale * activated * pre_up).astype(jnp.bfloat16)
    back_hidden = scale * jnp.einsum(
        "erd,efd->erf", back_arrived, weight_down, preferred_element_type=jnp.float32
    )
    back_up = (back_hidden * activated).astype(jnp.bfloat16)
    back_gate = (back_hidden * pre_up * sigma * (1.0 + pre_gate * (1.0 - sigma))).astype(
        jnp.bfloat16
    )
    grad_gate = jnp.einsum(
        "erd,erf->edf", token_arrived, back_gate, preferred_element_type=jnp.float32
    ).astype(jnp.bfloat16)
    grad_up = jnp.einsum(
        "erd,erf->edf", token_arrived, back_up, preferred_element_type=jnp.float32
    ).astype(jnp.bfloat16)
    grad_down = jnp.einsum(
        "erf,erd->efd", scaled_hidden, back_arrived, preferred_element_type=jnp.float32
    ).astype(jnp.bfloat16)
    up_term = jnp.einsum("edf,erf->der", weight_up, back_up, preferred_element_type=jnp.float32)
    gate_term = jnp.einsum(
        "edf,erf->der", weight_gate, back_gate, preferred_element_type=jnp.float32
    )
    slot_back = lax.psum_scatter(
        (up_term + gate_term).astype(jnp.bfloat16), "dp", scatter_dimension=0, tiled=True
    )
    returned = lax.all_to_all(slot_back, "expert", split_axis=2, concat_axis=1, tiled=True)
    flat_back = returned.reshape(quarter, experts * capacity)
    picked = (
        jnp.take(flat_back, slot_index, axis=1)
        .astype(jnp.float32)
        .reshape(quarter, token_rows, top_count)
    )
    grad_tokens = jnp.sum(picked, axis=2).T.astype(jnp.bfloat16)
    return (grad_tokens, grad_gate, grad_up, grad_down)


def solution(mesh):
    placed = (
        P("expert", None),
        P("expert", None),
        P("expert", None),
        P("expert", None),
        P("expert", None, "dp"),
        P("expert", None, "dp"),
        P("expert", "dp", None),
    )
    return jax.shard_map(
        per_device,
        mesh=mesh,
        in_specs=placed,
        out_specs=(
            P("expert", "dp"),
            P("expert", None, "dp"),
            P("expert", None, "dp"),
            P("expert", "dp", None),
        ),
        check_vma=False,
    )
```

profile of v0, /device:TPU:0, one launch (start us, length us, event | category | flops | bytes accessed | tf_op | source)
XLA Modules:
  0.0 770.3 jit_solution(8576594936999472891)
XLA Ops:
  7.2 0.7 broadcast_multiply_fusion
  7.8 0.8 copy.30
  8.6 0.1 eq.26
  8.8 0.1 reshape.180
  8.9 0.8 copy.34
  9.7 0.1 reshape.182
  9.9 0.1 copy.35
  10.0 0.1 mul.69
  10.1 0.6 reduce-window.6
  10.7 0.2 slice_reduce_fusion
  11.0 0.1 fusion.21
  11.1 1.4 scatter_custom_fusion
  12.5 5.0 gather_fusion
  17.5 0.7 all_to_all.16
  18.2 7.3 all-to-all-start
  25.5 1.7 concatenate.11
  27.2 9.4 %gather_fusion.2 = bf16[768,7168]{1,0:T(8,128)(2,1)} fusion(bf16[129,7168]{1,0:T(8,128)(2,1)S(1)} %concatenate.11, s32[1024]{0:T(1024)S(1)} %get-tuple-element.9), kind=kCustom, calls=%fused_computation.2 | custom fusion | bytes 22023168 | tf_op jit(solution)/shard_map/gather | solution.py:28
  36.6 0.0 all-to-all-done
  36.6 6.0 all-to-all-start.2
  42.6 1.7 concatenate.10
  44.3 9.5 %gather_fusion.1 = bf16[768,7168]{1,0:T(8,128)(2,1)} fusion(bf16[129,7168]{1,0:T(8,128)(2,1)S(1)} %concatenate.10, s32[1024]{0:T(1024)S(1)} %get-tuple-element.9), kind=kCustom, calls=%fused_computation.1 | custom fusion | bytes 22023168 | tf_op jit(solution)/shard_map/gather | solution.py:28
  53.7 227.6 %all-to-all-done.2 = bf16[8,96,7168]{2,1,0:T(8,128)(2,1)} async-done(((bf16[8,96,7168]{2,1,0:T(8,128)(2,1)}), bf16[8,96,7168]{2,1,0:T(8,128)(2,1)}, u32[]{:S(2)}, u32[]{:S(2)}) %all-to-all-start.2) | async-done | bytes 11010080 | tf_op jit(solution)/shard_map/all_to_all | solution.py:47
  281.4 5.2 all-to-all-start.1
  286.6 0.3 reduce-scatter.2.cloned.1.call-start
  286.9 0.1 reshape.191
  287.0 6.9 fusion.4
  293.9 230.6 %all-to-all-done.1 = bf16[8,96,7168]{2,1,0:T(8,128)(2,1)} async-done(((bf16[8,96,7168]{2,1,0:T(8,128)(2,1)}), bf16[8,96,7168]{2,1,0:T(8,128)(2,1)}, u32[]{:S(2)}, u32[]{:S(2)}) %all-to-all-start.1) | async-done | bytes 11010080 | tf_op jit(solution)/shard_map/all_to_all | solution.py:48
  524.5 0.0 copy-start.1
  524.5 7.1 fusion.13
  531.6 0.0 copy-done.1
  531.6 0.0 copy-start
  531.6 8.3 %multiply_convert_fusion.1 = (bf16[768,256]{1,0:T(8,128)(2,1)S(1)}, bf16[768,256]{1,0:T(8,128)(2,1)S(1)}, f32[768,256]{1,0:T(8,128)}) fusion(f32[768,256]{1,0:T(8,128)S(1)} %fusion.13, f32[768,256]{1,0:T(8,128)S(1)} %fusion.4, bf16[768,7168]{1,0:T(8,128)(2,1)} %bitcast.8, bf16[1,7168,256]{2,1,0:T(8,128)(2,1)S(1)} %copy-done.1), kind=kOutput, calls=%fused_computation.27 | convolution fusion | flops 2821128192 | bytes 17825792 | tf_op jit(solution)/shard_map/erd,edf->erf/dot_general | solution.py:52
  540.0 0.0 copy-start.4
  540.0 0.0 copy-start.2
  540.0 0.0 copy-done
  540.0 9.1 %fusion.6 = f32[768,7168]{1,0:T(8,128)} fusion(bf16[768,256]{1,0:T(8,128)(2,1)S(1)} %get-tuple-element.5, bf16[1,7168,256]{2,1,0:T(8,128)(2,1)S(1)} %copy-done), kind=kOutput, calls=%fused_computation.15 | convolution fusion | flops 2818572288 | bytes 26083328 | tf_op jit(solution)/shard_map/edf,erf->der/dot_general | solution.py:77
  549.0 0.0 copy-done.4
  549.0 0.0 copy-done.2
  549.0 12.8 %fusion = bf16[7168,1,768]{0,2,1:T(8,128)(2,1)} fusion(f32[768,7168]{1,0:T(8,128)} %fusion.6, bf16[768,256]{1,0:T(8,128)(2,1)S(1)} %get-tuple-element.4, bf16[1,7168,256]{2,1,0:T(8,128)(2,1)S(1)} %copy-done.1), kind=kOutput, calls=%fused_computation.6 | convolution fusion | flops 2829582336 | bytes 37093376 | tf_op jit(solution)/shard_map/edf,erf->der/dot_general | solution.py:78
  561.9 0.0 reduce-scatter.2.cloned.1.call-update
  561.9 88.4 %reduce-scatter.2.cloned.1.call-done = bf16[1792,1,768]{0,2,1:T(8,128)(2,1)} async-done(((bf16[7168,1,768]{0,2,1:T(8,128)(2,1)}), bf16[1792,1,768]{0,2,1:T(8,128)(2,1)}) %reduce-scatter.2.cloned.1.call-update) | async-done | bytes 2752528 | tf_op jit(solution)/shard_map/reduce_scatter | solution.py:81
  650.3 8.4 %copy.44 = bf16[1792,1,768]{0,1,2:T(2,128)(2,1)} copy(bf16[1792,1,768]{0,2,1:T(8,128)(2,1)} %reduce-scatter.2.cloned.1.call-done) | data formatting | bytes 5505024 | tf_op jit(solution)/shard_map/reduce_scatter | solution.py:81
  658.7 0.5 broadcast.118
  659.2 17.0 %reduce.7 = bf16[768,1792]{1,0:T(8,128)(2,1)S(1)} reduce(bf16[768,1,1792]{2,1,0:T(2,128)(2,1)} %bitcast.67, bf16[]{:T(256)} %broadcast.118), dimensions={1}, to_apply=%bitcast.62.reduce_sub_computation | reduce | bytes 5505026
  676.2 0.0 copy-start.7
  676.3 3.5 reshape.245
  679.7 5.7 all-to-all-start.3
  685.4 0.8 reduce_sum.26
  686.2 0.9 copy.32
  687.1 0.0 copy-done.7
  687.1 0.5 compare_and_fusion
  687.6 1.4 copy.33
  689.0 9.5 %fusion.3 = bf16[1,256,7168]{2,1,0:T(8,128)(2,1)} fusion(bf16[768,7168]{1,0:T(8,128)(2,1)} %bitcast.5, f32[768,256]{1,0:T(8,128)S(1)} %fusion.4, f32[768]{0:T(1024)S(1)} %reshape.191, f32[768,256]{1,0:T(8,128)} %get-tuple-element.8), kind=kOutput, calls=%fused_computation.12 | convolution fusion | flops 2821783552 | bytes 16256000 | tf_op jit(solution)/shard_map/erf,erd->efd/dot_general | solution.py:74
  698.5 0.0 copy-done.3
  698.5 9.1 %fusion.1 = bf16[1,7168,256]{2,1,0:T(8,128)(2,1)} fusion(bf16[768,7168]{1,0:T(8,128)(2,1)} %bitcast.8, bf16[768,256]{1,0:T(8,128)(2,1)S(1)} %copy-done.3), kind=kOutput, calls=%fused_computation.10 | convolution fusion | flops 2820407296 | bytes 15073280 | tf_op jit(solution)/shard_map/erd,erf->edf/dot_general | solution.py:68
  707.6 0.0 copy-done.5
  707.6 9.1 %fusion.2 = bf16[1,7168,256]{2,1,0:T(8,128)(2,1)} fusion(bf16[768,7168]{1,0:T(8,128)(2,1)} %bitcast.8, bf16[768,256]{1,0:T(8,128)(2,1)S(1)} %copy-done.5), kind=kOutput, calls=%fused_computation.11 | convolution fusion | flops 2820407296 | bytes 15073280 | tf_op jit(solution)/shard_map/erd,erf->edf/dot_general | solution.py:71
  716.7 31.0 %all-to-all-done.3 = bf16[8,2,86016]{2,1,0:T(2,128)(2,1)S(1)} async-done(((bf16[8,2,86016]{2,1,0:T(2,128)(2,1)}), bf16[8,2,86016]{2,1,0:T(2,128)(2,1)S(1)}, u32[]{:S(2)}, u32[]{:S(2)}) %all-to-all-start.3) | async-done | bytes 2752544 | tf_op jit(solution)/shard_map/all_to_all | solution.py:84
  747.7 4.9 reshape.246
  752.6 3.0 copy.43
  755.6 2.3 gather_fusion.3
  757.9 2.5 gather.19
  760.4 0.0 copy-done.6
  760.4 2.8 fusion.16
  (13 shorter events, 0.1 us)
Async XLA Ops:
  18.2 18.3 %all-to-all-start = ((bf16[8,1,96]{2,1,0:T(2,128)(2,1)}), bf16[8,1,96]{2,1,0:T(2,128)(2,1)S(1)}, u32[]{:S(2)}, u32[]{:S(2)}) async-start(bf16[8,1,96]{2,1,0:T(2,128)(2,1)} %all_to_all.16), calls=%async_computation | async-start | bytes 8192 | tf_op jit(solution)/shard_map/all_to_all | solution.py:49
  36.6 244.8 %all-to-all-start.2 = ((bf16[8,96,7168]{2,1,0:T(8,128)(2,1)}), bf16[8,96,7168]{2,1,0:T(8,128)(2,1)}, u32[]{:S(2)}, u32[]{:S(2)}) async-start(bf16[8,96,7168]{2,1,0:T(8,128)(2,1)} %bitcast.65), calls=%async_computation.2 | async-start | bytes 22020096 | tf_op jit(solution)/shard_map/all_to_all | solution.py:47
  281.4 243.2 %all-to-all-start.1 = ((bf16[8,96,7168]{2,1,0:T(8,128)(2,1)}), bf16[8,96,7168]{2,1,0:T(8,128)(2,1)}, u32[]{:S(2)}, u32[]{:S(2)}) async-start(bf16[8,96,7168]{2,1,0:T(8,128)(2,1)} %bitcast.64), calls=%async_computation.1 | async-start | bytes 22020096 | tf_op jit(solution)/shard_map/all_to_all | solution.py:48
  286.6 363.7 %reduce-scatter.2.cloned.1.call-start = ((), (), s32[]{:S(2)}) async-start(), calls=%async_computation.5 | async-start | bytes 13762560 | tf_op jit(solution)/shard_map/reduce_scatter | solution.py:81
  524.5 7.1 copy-start.1
  531.6 8.3 %copy-start = (bf16[1,7168,256]{2,1,0:T(8,128)(2,1)S(1)}, bf16[1,7168,256]{2,1,0:T(8,128)(2,1)}, u32[]{:S(2)}) copy-start(bf16[1,7168,256]{2,1,0:T(8,128)(2,1)} %param.12) | copy-start | bytes 11010052
  540.0 9.1 %copy-start.4 = (bf16[768,256]{1,0:T(8,128)(2,1)}, bf16[768,256]{1,0:T(8,128)(2,1)S(1)}, u32[]{:S(2)}) copy-start(bf16[768,256]{1,0:T(8,128)(2,1)S(1)} %get-tuple-element.5) | copy-start | bytes 1179652
  540.0 9.1 %copy-start.2 = (bf16[768,256]{1,0:T(8,128)(2,1)}, bf16[768,256]{1,0:T(8,128)(2,1)S(1)}, u32[]{:S(2)}) copy-start(bf16[768,256]{1,0:T(8,128)(2,1)S(1)} %get-tuple-element.4) | copy-start | bytes 1179652
  676.2 10.9 %copy-start.7 = (s32[128,2]{0,1:T(2,128)S(1)}, s32[128,2]{0,1:T(2,128)}, u32[]{:S(2)}) copy-start(s32[128,2]{0,1:T(2,128)} %param.8) | copy-start | bytes 3076
  679.7 68.0 %all-to-all-start.3 = ((bf16[8,2,86016]{2,1,0:T(2,128)(2,1)}), bf16[8,2,86016]{2,1,0:T(2,128)(2,1)S(1)}, u32[]{:S(2)}, u32[]{:S(2)}) async-start(bf16[8,2,86016]{2,1,0:T(2,128)(2,1)} %reshape.245), calls=%async_computation.4 | async-start | bytes 5505024 | tf_op jit(solution)/shard_map/all_to_all | solution.py:84
  689.0 9.5 %copy-start.3 = (bf16[768,256]{1,0:T(8,128)(2,1)S(1)}, bf16[768,256]{1,0:T(8,128)(2,1)}, u32[]{:S(2)}) copy-start(bf16[768,256]{1,0:T(8,128)(2,1)} %copy-done.2) | copy-start | bytes 1179652
  698.5 9.1 %copy-start.5 = (bf16[768,256]{1,0:T(8,128)(2,1)S(1)}, bf16[768,256]{1,0:T(8,128)(2,1)}, u32[]{:S(2)}) copy-start(bf16[768,256]{1,0:T(8,128)(2,1)} %copy-done.4) | copy-start | bytes 1179652
  752.6 7.8 %copy-start.6 = (pred[128,2]{1,0:T(8,128)(4,1)S(1)}, pred[128,2]{1,0:T(8,128)(4,1)}, u32[]{:S(2)}) copy-start(pred[128,2]{1,0:T(8,128)(4,1)} %copy.33) | copy-start | bytes 772
Sparse Core Ops, SparseCore 0:
  562.0 88.2 reduce-scatter.1
where the time goes:
time: 776 us; the launch traced here: 770 us
  waiting for transfers between devices  578 us (74%)
  matrix products  71.9 us (9%)
  local copies, waits for them, and re-layouts  60 us (8%)
  starting transfers between devices  24.5 us (3%)
  other arithmetic  21.8 us (3%)
  between operations  14.5 us (2%)
    all_to_all x1, waiting for transfers between devices, per_device(): lax.all_to_all(back_send, 'expert', split_axis=0, concat_axis=1, tiled=True)  231 us
    all_to_all x1, waiting for transfers between devices, per_device(): lax.all_to_all(token_send, 'expert', split_axis=0, concat_axis=1, tiled=T...  228 us
    reduce_scatter x1, waiting for transfers between devices, per_device(): lax.psum_scatter((up_term + gate_term).astype(jnp.bfloat16), 'dp', scatte...  88.4 us
    all_to_all x1, waiting for transfers between devices, per_device(): lax.all_to_all(slot_back, 'expert', split_axis=2, concat_axis=1, tiled=True)  31 us
    gather x2, local copies, waits for them, and re-layouts, pad_rows(): return extended[owners // top_count]  18.9 us
    unnamed x1, other arithmetic  17 us
  transfers between devices with their start and end apart: 5, of which 4 were waited for; matrix products, arithmetic and copies ran while one was open for 8% of the time, Pallas kernels for 0%

commit v1 on v0

--- a/solution.py
+++ b/solution.py
@@ -2,6 +2,22 @@
 import jax.numpy as jnp
 from jax import lax
 from jax.sharding import PartitionSpec as P
+
+
+def swapped_with_each(value, axis, split, join):
+    ways, here = (lax.axis_size(axis), lax.axis_index(axis))
+    width = value.shape[split] // ways
+    dims = list(value.shape)
+    dims[split] = width
+    height = dims[join]
+    dims[join] = height * ways
+    full = jnp.zeros(dims, value.dtype)
+    for mask in range(ways):
+        part = lax.dynamic_slice_in_dim(value, (here ^ mask) * width, width, axis=split)
+        if mask:
+            part = lax.ppermute(part, axis, [(d, d ^ mask) for d in range(ways)])
+        full = lax.dynamic_update_slice_in_dim(full, part, (here ^ mask) * height, axis=join)
+    return full
 
 
 def slot_layout(routes, experts, capacity):
@@ -81,7 +97,7 @@
     slot_back = lax.psum_scatter(
         (up_term + gate_term).astype(jnp.bfloat16), "dp", scatter_dimension=0, tiled=True
     )
-    returned = lax.all_to_all(slot_back, "expert", split_axis=2, concat_axis=1, tiled=True)
+    returned = swapped_with_each(slot_back, "expert", 2, 1)
     flat_back = returned.reshape(quarter, experts * capacity)
     picked = (
         jnp.take(flat_back, slot_index, axis=1)

time: 776 us -> 745 us (0.960)
  local copies, waits for them, and re-layouts: 60 us -> 39.9 us
  other arithmetic: 21.8 us -> 4.29 us
    ppermute x0 -> x7, waiting for transfers between devices: none -> 58.3 us  [swapped_with_each(): part = lax.ppermute(part, axis, [(d, d ^ mask) for d in range(ways)])]
    all_to_all x1 -> x0, waiting for transfers between devices: 31 us -> none  [per_device(): lax.all_to_all(slot_back, 'expert', split_axis=2, concat_axis=1, tiled=True)]
    reduce_scatter x1, waiting for transfers between devices: 88.4 us -> 65.7 us  [per_device(): lax.psum_scatter((up_term + gate_term).astype(jnp.bfloat16), 'dp', scatte...]
    unnamed x1 -> x0, other arithmetic: 17 us -> none
    ppermute x0 -> x7, starting transfers between devices: none -> 10.8 us  [swapped_with_each(): part = lax.ppermute(part, axis, [(d, d ^ mask) for d in range(ways)])]
    reduce_scatter x1 -> x0, local copies, waits for them, and re-layouts: 8.41 us -> none  [per_device(): lax.psum_scatter((up_term + gate_term).astype(jnp.bfloat16), 'dp', scatte...]
  transfers between devices with their start and end apart: 5 -> 11, of which waited for: 4 -> 5; matrix products, arithmetic and copies ran while one was open for 8% -> 8% of each run, Pallas kernels for 0% -> 0%
where the time goes in v1:
time: 745 us; the launch traced here: 744 us
  waiting for transfers between devices  582 us (78%)
  matrix products  73.9 us (10%)
  local copies, waits for them, and re-layouts  39.9 us (5%)
  starting transfers between devices  29.5 us (4%)
  between operations  14.4 us (2%)
    all_to_all x1, waiting for transfers between devices, per_device(): lax.all_to_all(back_send, 'expert', split_axis=0, concat_axis=1, tiled=True)  231 us
    all_to_all x1, waiting for transfers between devices, per_device(): lax.all_to_all(token_send, 'expert', split_axis=0, concat_axis=1, tiled=T...  228 us
    reduce_scatter x1, waiting for transfers between devices, per_device(): lax.psum_scatter((up_term + gate_term).astype(jnp.bfloat16), 'dp', scatte...  65.7 us
    ppermute x7, waiting for transfers between devices, swapped_with_each(): part = lax.ppermute(part, axis, [(d, d ^ mask) for d in range(ways)])  58.3 us
    gather x2, local copies, waits for them, and re-layouts, pad_rows(): return extended[owners // top_count]  18.8 us
  transfers between devices with their start and end apart: 11, of which 5 were waited for; matrix products, arithmetic and copies ran while one was open for 8% of the time, Pallas kernels for 0%

profile of v1, /device:TPU:0, one launch (start us, length us, event | category | flops | bytes accessed | tf_op | source)
XLA Modules:
  0.0 744.4 jit_solution(1938303001867056463)
XLA Ops:
  7.2 0.7 broadcast_multiply_fusion
  7.8 0.8 copy.21
  8.6 0.1 eq.26
  8.8 0.1 reshape.176
  8.9 0.8 copy.25
  9.7 0.1 reshape.178
  9.9 0.1 copy.26
  10.0 0.1 mul.93
  10.1 0.6 reduce-window.6
  10.7 0.2 slice_reduce_fusion
  11.0 0.1 fusion.21
  11.1 1.4 scatter_custom_fusion
  12.5 5.0 gather_fusion
  17.5 0.7 all_to_all.13
  18.2 7.3 all-to-all-start
  25.5 1.7 concatenate.11
  27.2 9.4 %gather_fusion.2 = bf16[768,7168]{1,0:T(8,128)(2,1)} fusion(bf16[129,7168]{1,0:T(8,128)(2,1)S(1)} %concatenate.11, s32[1024]{0:T(1024)S(1)} %get-tuple-element.17), kind=kCustom, calls=%fused_computation.2 | custom fusion | bytes 22023168 | tf_op jit(solution)/shard_map/gather | solution.py:44
  36.5 0.0 all-to-all-done
  36.5 6.0 all-to-all-start.2
  42.5 1.7 concatenate.10
  44.2 9.5 %gather_fusion.1 = bf16[768,7168]{1,0:T(8,128)(2,1)} fusion(bf16[129,7168]{1,0:T(8,128)(2,1)S(1)} %concatenate.10, s32[1024]{0:T(1024)S(1)} %get-tuple-element.17), kind=kCustom, calls=%fused_computation.1 | custom fusion | bytes 22023168 | tf_op jit(solution)/shard_map/gather | solution.py:44
  53.7 227.6 %all-to-all-done.2 = bf16[8,96,7168]{2,1,0:T(8,128)(2,1)} async-done(((bf16[8,96,7168]{2,1,0:T(8,128)(2,1)}), bf16[8,96,7168]{2,1,0:T(8,128)(2,1)}, u32[]{:S(2)}, u32[]{:S(2)}) %all-to-all-start.2) | async-done | bytes 11010080 | tf_op jit(solution)/shard_map/all_to_all | solution.py:63
  281.3 5.2 all-to-all-start.1
  286.6 0.2 reduce-scatter.2.cloned.1.call-start
  286.8 0.1 reshape.187
  286.9 6.9 fusion.4
  293.8 230.7 %all-to-all-done.1 = bf16[8,96,7168]{2,1,0:T(8,128)(2,1)} async-done(((bf16[8,96,7168]{2,1,0:T(8,128)(2,1)}), bf16[8,96,7168]{2,1,0:T(8,128)(2,1)}, u32[]{:S(2)}, u32[]{:S(2)}) %all-to-all-start.1) | async-done | bytes 11010080 | tf_op jit(solution)/shard_map/all_to_all | solution.py:64
  524.5 7.1 fusion.13
  531.6 0.0 copy-done.1
  531.6 0.0 copy-start
  531.6 8.3 %multiply_convert_fusion.1 = (bf16[768,256]{1,0:T(8,128)(2,1)S(1)}, bf16[768,256]{1,0:T(8,128)(2,1)S(1)}, f32[768,256]{1,0:T(8,128)}) fusion(f32[768,256]{1,0:T(8,128)S(1)} %fusion.13, f32[768,256]{1,0:T(8,128)S(1)} %fusion.4, bf16[768,7168]{1,0:T(8,128)(2,1)} %bitcast.8, bf16[1,7168,256]{2,1,0:T(8,128)(2,1)S(1)} %copy-done.1), kind=kOutput, calls=%fused_computation.26 | convolution fusion | flops 2821128192 | bytes 17825792 | tf_op jit(solution)/shard_map/erd,edf->erf/dot_general | solution.py:68
  539.9 9.1 %fusion.6 = f32[768,7168]{1,0:T(8,128)} fusion(bf16[768,256]{1,0:T(8,128)(2,1)S(1)} %get-tuple-element.13, bf16[1,7168,256]{2,1,0:T(8,128)(2,1)S(1)} %copy-done), kind=kOutput, calls=%fused_computation.15 | convolution fusion | flops 2818572288 | bytes 26083328 | tf_op jit(solution)/shard_map/edf,erf->der/dot_general | solution.py:93
  549.0 12.4 %fusion = bf16[7168,1,768]{0,2,1:T(8,128)(2,1)} fusion(f32[768,7168]{1,0:T(8,128)} %fusion.6, bf16[768,256]{1,0:T(8,128)(2,1)S(1)} %get-tuple-element.12, bf16[1,7168,256]{2,1,0:T(8,128)(2,1)S(1)} %copy-done.1), kind=kOutput, calls=%fused_computation.6 | convolution fusion | flops 2829582336 | bytes 37093376 | tf_op jit(solution)/shard_map/edf,erf->der/dot_general | solution.py:94
  561.4 0.0 reduce-scatter.2.cloned.1.call-update
  561.5 0.1 reduce_sum.26
  561.6 0.1 copy.23
  561.7 0.4 copy-done.7
  562.1 0.7 copy.24
  562.8 10.1 %fusion.1 = bf16[1,7168,256]{2,1,0:T(8,128)(2,1)} fusion(bf16[768,7168]{1,0:T(8,128)(2,1)} %bitcast.8, bf16[768,256]{1,0:T(8,128)(2,1)S(1)} %get-tuple-element.12), kind=kOutput, calls=%fused_computation.10 | convolution fusion | flops 2820407296 | bytes 15073280 | tf_op jit(solution)/shard_map/erd,erf->edf/dot_general | solution.py:84
  572.9 11.1 %fusion.2 = bf16[1,7168,256]{2,1,0:T(8,128)(2,1)} fusion(bf16[768,7168]{1,0:T(8,128)(2,1)} %bitcast.8, bf16[768,256]{1,0:T(8,128)(2,1)S(1)} %copy-done.5), kind=kOutput, calls=%fused_computation.11 | convolution fusion | flops 2820407296 | bytes 15073280 | tf_op jit(solution)/shard_map/erd,erf->edf/dot_general | solution.py:87
  584.0 65.7 %reduce-scatter.2.cloned.1.call-done = bf16[1792,1,768]{0,2,1:T(8,128)(2,1)} async-done(((bf16[7168,1,768]{0,2,1:T(8,128)(2,1)}), bf16[1792,1,768]{0,2,1:T(8,128)(2,1)}) %reduce-scatter.2.cloned.1.call-update) | async-done | bytes 2752528 | tf_op jit(solution)/shard_map/reduce_scatter | solution.py:97
  649.7 0.2 broadcast_in_dim.27
  649.9 1.6 copy-done.2
  651.5 0.2 constant_dynamic-slice_fusion
  651.7 1.6 collective-permute-start.1
  653.3 1.5 collective-permute-start
  654.7 0.0 copy-done.3
  654.7 9.0 %fusion.3 = bf16[1,256,7168]{2,1,0:T(8,128)(2,1)} fusion(bf16[768,7168]{1,0:T(8,128)(2,1)} %bitcast.5, f32[768,256]{1,0:T(8,128)S(1)} %fusion.4, f32[768]{0:T(1024)S(1)} %reshape.187, f32[768,256]{1,0:T(8,128)S(1)} %copy-done.3), kind=kOutput, calls=%fused_computation.12 | convolution fusion | flops 2821783552 | bytes 16256000 | tf_op jit(solution)/shard_map/erf,erd->efd/dot_general | solution.py:90
  663.7 2.4 collective-permute-start.6
  666.1 1.5 collective-permute-start.5
  667.5 1.5 collective-permute-start.4
  669.0 0.0 collective-permute-done
  669.0 2.3 collective-permute-start.2
  671.4 0.0 collective-permute-done.1
  671.4 0.1 collective-permute-start.3
  671.5 29.0 %collective-permute-done.2 = bf16[1792,1,96]{0,2,1:T(8,128)(2,1)S(1)} collective-permute-done((bf16[1792,1,96]{0,2,1:T(8,128)(2,1)S(1)}, bf16[1792,1,96]{0,2,1:T(8,128)(2,1)S(1)}, u32[]{:S(2)}, u32[]{:S(2)}) %collective-permute-start.2) | collective-permute-done | bytes 344096 | tf_op jit(solution)/shard_map/ppermute | solution.py:18
  700.6 29.3 %collective-permute-done.3 = bf16[1792,1,96]{0,2,1:T(8,128)(2,1)S(1)} collective-permute-done((bf16[1792,1,96]{0,2,1:T(8,128)(2,1)S(1)}, bf16[1792,1,96]{0,2,1:T(8,128)(2,1)S(1)}, u32[]{:S(2)}, u32[]{:S(2)}) %collective-permute-start.3) | collective-permute-done | bytes 344096 | tf_op jit(solution)/shard_map/ppermute | solution.py:18
  729.9 0.0 collective-permute-done.4
  730.0 0.0 collective-permute-done.5
  730.0 0.0 collective-permute-done.6
  730.1 2.3 gather_fusion.3
  732.4 2.3 gather.19
  734.7 0.0 copy-done.6
  734.7 2.8 fusion.16
  (28 shorter events, 0.3 us)
Async XLA Ops:
  18.2 18.3 %all-to-all-start = ((bf16[8,1,96]{2,1,0:T(2,128)(2,1)}), bf16[8,1,96]{2,1,0:T(2,128)(2,1)S(1)}, u32[]{:S(2)}, u32[]{:S(2)}) async-start(bf16[8,1,96]{2,1,0:T(2,128)(2,1)} %all_to_all.13), calls=%async_computation | async-start | bytes 8192 | tf_op jit(solution)/shard_map/all_to_all | solution.py:65
  36.5 244.8 %all-to-all-start.2 = ((bf16[8,96,7168]{2,1,0:T(8,128)(2,1)}), bf16[8,96,7168]{2,1,0:T(8,128)(2,1)}, u32[]{:S(2)}, u32[]{:S(2)}) async-start(bf16[8,96,7168]{2,1,0:T(8,128)(2,1)} %bitcast.58), calls=%async_computation.2 | async-start | bytes 22020096 | tf_op jit(solution)/shard_map/all_to_all | solution.py:63
  281.3 243.2 %all-to-all-start.1 = ((bf16[8,96,7168]{2,1,0:T(8,128)(2,1)}), bf16[8,96,7168]{2,1,0:T(8,128)(2,1)}, u32[]{:S(2)}, u32[]{:S(2)}) async-start(bf16[8,96,7168]{2,1,0:T(8,128)(2,1)} %bitcast.57), calls=%async_computation.1 | async-start | bytes 22020096 | tf_op jit(solution)/shard_map/all_to_all | solution.py:64
  286.6 363.2 %reduce-scatter.2.cloned.1.call-start = ((), (), s32[]{:S(2)}) async-start(), calls=%async_computation.4 | async-start | bytes 13762560 | tf_op jit(solution)/shard_map/reduce_scatter | solution.py:97
  524.5 7.1 copy-start.1
  531.6 8.3 %copy-start = (bf16[1,7168,256]{2,1,0:T(8,128)(2,1)S(1)}, bf16[1,7168,256]{2,1,0:T(8,128)(2,1)}, u32[]{:S(2)}) copy-start(bf16[1,7168,256]{2,1,0:T(8,128)(2,1)} %param.12) | copy-start | bytes 11010052
  539.9 9.1 %copy-start.4 = (bf16[768,256]{1,0:T(8,128)(2,1)}, bf16[768,256]{1,0:T(8,128)(2,1)S(1)}, u32[]{:S(2)}) copy-start(bf16[768,256]{1,0:T(8,128)(2,1)S(1)} %get-tuple-element.13) | copy-start | bytes 1179652
  561.4 0.7 copy-start.7
  562.8 10.1 %copy-start.5 = (bf16[768,256]{1,0:T(8,128)(2,1)S(1)}, bf16[768,256]{1,0:T(8,128)(2,1)}, u32[]{:S(2)}) copy-start(bf16[768,256]{1,0:T(8,128)(2,1)} %copy-done.4) | copy-start | bytes 1179652
  649.7 1.8 copy-start.2
  649.7 5.0 copy-start.3
  651.7 19.7 %collective-permute-start.1 = (bf16[1792,1,96]{0,2,1:T(8,128)(2,1)S(1)}, bf16[1792,1,96]{0,2,1:T(8,128)(2,1)S(1)}, u32[]{:S(2)}, u32[]{:S(2)}) collective-permute-start(bf16[1792,1,96]{0,2,1:T(8,128)(2,1)S(1)} %get-tuple-element.9), channel_id=1, source_target_pairs={{0,8},{4,12},{8,0},{12,4},{16,24},{20,28},{24,16},{28,20},{1,9},{5... | collective-permute-start | bytes 1032200 | tf_op jit(solution)/shard_map/ppermute | solution.py:18
  653.3 15.8 %collective-permute-start = (bf16[1792,1,96]{0,2,1:T(8,128)(2,1)S(1)}, bf16[1792,1,96]{0,2,1:T(8,128)(2,1)S(1)}, u32[]{:S(2)}, u32[]{:S(2)}) collective-permute-start(bf16[1792,1,96]{0,2,1:T(8,128)(2,1)S(1)} %get-tuple-element.10), channel_id=1, source_target_pairs={{0,4},{4,0},{8,12},{12,8},{16,20},{20,16},{24,28},{28,24},{1,5},{5... | collective-permute-start | bytes 1032200 | tf_op jit(solution)/shard_map/ppermute | solution.py:18
  663.7 66.3 %collective-permute-start.6 = (bf16[1792,1,96]{0,2,1:T(8,128)(2,1)S(1)}, bf16[1792,1,96]{0,2,1:T(8,128)(2,1)S(1)}, u32[]{:S(2)}, u32[]{:S(2)}) collective-permute-start(bf16[1792,1,96]{0,2,1:T(8,128)(2,1)S(1)} %get-tuple-element.4), channel_id=1, source_target_pairs={{0,28},{4,24},{8,20},{12,16},{16,12},{20,8},{24,4},{28,0},{1,29},{... | collective-permute-start | bytes 1032200 | tf_op jit(solution)/shard_map/ppermute | solution.py:18
  666.1 63.9 %collective-permute-start.5 = (bf16[1792,1,96]{0,2,1:T(8,128)(2,1)S(1)}, bf16[1792,1,96]{0,2,1:T(8,128)(2,1)S(1)}, u32[]{:S(2)}, u32[]{:S(2)}) collective-permute-start(bf16[1792,1,96]{0,2,1:T(8,128)(2,1)S(1)} %get-tuple-element.5), channel_id=1, source_target_pairs={{0,24},{4,28},{8,16},{12,20},{16,8},{20,12},{24,0},{28,4},{1,25},{... | collective-permute-start | bytes 1032200 | tf_op jit(solution)/shard_map/ppermute | solution.py:18
  667.5 62.4 %collective-permute-start.4 = (bf16[1792,1,96]{0,2,1:T(8,128)(2,1)S(1)}, bf16[1792,1,96]{0,2,1:T(8,128)(2,1)S(1)}, u32[]{:S(2)}, u32[]{:S(2)}) collective-permute-start(bf16[1792,1,96]{0,2,1:T(8,128)(2,1)S(1)} %get-tuple-element.6), channel_id=1, source_target_pairs={{0,20},{4,16},{8,28},{12,24},{16,4},{20,0},{24,12},{28,8},{1,21},{... | collective-permute-start | bytes 1032200 | tf_op jit(solution)/shard_map/ppermute | solution.py:18
  669.0 31.5 %collective-permute-start.2 = (bf16[1792,1,96]{0,2,1:T(8,128)(2,1)S(1)}, bf16[1792,1,96]{0,2,1:T(8,128)(2,1)S(1)}, u32[]{:S(2)}, u32[]{:S(2)}) collective-permute-start(bf16[1792,1,96]{0,2,1:T(8,128)(2,1)S(1)} %get-tuple-element.8), channel_id=1, source_target_pairs={{0,12},{4,8},{8,4},{12,0},{16,28},{20,24},{24,20},{28,16},{1,13},{... | collective-permute-start | bytes 1032200 | tf_op jit(solution)/shard_map/ppermute | solution.py:18
  671.4 58.5 %collective-permute-start.3 = (bf16[1792,1,96]{0,2,1:T(8,128)(2,1)S(1)}, bf16[1792,1,96]{0,2,1:T(8,128)(2,1)S(1)}, u32[]{:S(2)}, u32[]{:S(2)}) collective-permute-start(bf16[1792,1,96]{0,2,1:T(8,128)(2,1)S(1)} %get-tuple-element.7), channel_id=1, source_target_pairs={{0,16},{4,20},{8,24},{12,28},{16,0},{20,4},{24,8},{28,12},{1,17},{... | collective-permute-start | bytes 1032200 | tf_op jit(solution)/shard_map/ppermute | solution.py:18
  730.1 4.6 copy-start.6
Sparse Core Ops, SparseCore 0:
  561.6 88.1 reduce-scatter.1
